TPU v7x, 256 devices: a whole 4x4x8 slice. The times are simulated.
256 devices in a mesh: gx: 64 (over z, y, x_hi), gy: 4 (over x_lo, core).
Axes of the slice: x: 4 (x_hi: 2, x_lo: 2; x = x_hi * 2 + x_lo), y: 4, z: 8, core: 2. Of those that a mesh axis runs over, the one named last changes fastest.
Arguments:
- points: bfloat16 [4, 64, 64, 32, 128], P('gy', 'gx'), may hold values from -6 to 6
- counts: int32 [4, 64, 64], P('gy', 'gx'), may hold values from 10 to 32, as said below
- voxels: int32 [4, 64, 64, 32], P('gy', 'gx'), may hold values from 0 to 1023, as said below
- occupancy: int32 [64, 4, 2], P('gx', 'gy'), may hold values from 0 to 1, as said below
- weight: bfloat16 [27, 96, 96], replicated, may hold values from -0.125 to 0.125
- w_in: bfloat16 [128, 96], replicated, may hold values from -0.5 to 0.5
- cotangent: bfloat16 [512, 32, 16, 96], P('gx', 'gy'), may hold values from -6 to 6
Outputs:
- point_feat: bfloat16 [4, 64, 64, 32, 96], P('gy', 'gx')
- point_grad: bfloat16 [4, 64, 64, 32, 128], P('gy', 'gx')
- weight_grad: float32 [27, 96, 96], replicated
Inputs may be any that keep to these rules, and one draw needn't show every extreme that they name: `counts`: in each gy row one owner receives 32 rows from every source. `voxels`: every slot's voxel lies in an occupied block of its owner tile. `occupancy`: every tile has at least one occupied block.
All inputs are finite; a program needn't handle non-finite values.
Results may differ from a plain program's by a relative error of at most 0.01.
Values may be sent and summed in bfloat16 or wider, within the bound.
A program may use at most 64 MiB of HBM per device.

v0:
```python
import jax
import jax.numpy as jnp
from jax import lax
from jax.sharding import PartitionSpec as P


def padded_2(block, sides, width):
    for axis, dim in sides:
        count = lax.axis_size(axis)
        forward = [(i, i + 1) for i in range(count - 1)]
        backward = [(target, source) for source, target in forward]
        low = lax.ppermute(
            lax.slice_in_dim(block, block.shape[dim] - width, None, axis=dim), axis, forward
        )
        high = lax.ppermute(lax.slice_in_dim(block, 0, width, axis=dim), axis, backward)
        block = jnp.concatenate([low, block, high], axis=dim)
    return block


def pad_depth(field):
    return jnp.pad(field, ((0, 0), (0, 0), (1, 1), (0, 0)))


def forward_taps(padded, weight, depth, width):
    total = jnp.zeros((64 * depth, width), jnp.float32)
    for tap in range(27):
        a, b, c = (tap // 9, tap // 3 % 3, tap % 3)
        window = padded[a : a + 8, b : b + 8, c : c + depth].reshape(-1, width)
        total = total + jnp.dot(window, weight[tap], preferred_element_type=jnp.float32)
    return total


def weight_terms(padded, grad_flat, depth, width):
    terms = []
    for tap in range(27):
        a, b, c = (tap // 9, tap // 3 % 3, tap % 3)
        window = padded[a : a + 8, b : b + 8, c : c + depth].reshape(-1, width)
        terms.append(
            lax.dot_general(
                window, grad_flat, (((0,), (0,)), ((), ())), preferred_element_type=jnp.float32
            )
        )
    return jnp.stack(terms)


def backward_taps(padded, weight, depth, width):
    total = jnp.zeros((64 * depth, width), jnp.float32)
    for tap in range(27):
        a, b, c = (tap // 9, tap // 3 % 3, tap % 3)
        window = padded[2 - a : 10 - a, 2 - b : 10 - b, 2 - c : 2 - c + depth].reshape(-1, width)
        total = total + jnp.dot(window, weight[tap].T, preferred_element_type=jnp.float32)
    return total


def on_device(points, counts, voxels, occupancy, weight, w_in, cotangent):
    width = weight.shape[2]
    feat_width = points.shape[4]
    depth = cotangent.shape[2]
    shape_slots = voxels.shape
    slots = lax.broadcasted_iota(jnp.int32, shape_slots, 3)
    got_points, got_voxels, got_counts = (
        lax.all_to_all(points, "gx", split_axis=2, concat_axis=2, tiled=True),
        lax.all_to_all(voxels, "gx", split_axis=2, concat_axis=2, tiled=True),
        lax.all_to_all(counts, "gx", split_axis=2, concat_axis=2, tiled=True),
    )
    got_valid = (slots < got_counts[..., None]).astype(jnp.float32).reshape(-1, 1)
    proj = (
        jnp.dot(got_points.reshape(-1, feat_width), w_in, preferred_element_type=jnp.float32)
        * got_valid
    ).astype(jnp.bfloat16)
    flat_index = got_voxels.reshape(-1)
    column_mask = jnp.repeat(occupancy[0, 0], 8).astype(jnp.float32)
    mask = jnp.broadcast_to(column_mask[None, None, :, None], (8, 8, depth, 1))
    summed = (
        jnp.zeros((64 * depth, width), jnp.float32).at[flat_index].add(proj.astype(jnp.float32))
    )
    feature = (summed.reshape(8, 8, depth, width) * mask).astype(jnp.bfloat16)
    grad_masked = (cotangent.astype(jnp.float32) * mask).astype(jnp.bfloat16)
    feature_pad = pad_depth(padded_2(feature, (("gx", 0), ("gy", 1)), 1))
    grad_pad = pad_depth(padded_2(grad_masked, (("gx", 0), ("gy", 1)), 1))
    mask_flat = mask.reshape(-1, 1)
    output = (forward_taps(feature_pad, weight, depth, width) * mask_flat).astype(jnp.bfloat16)
    local_grad = weight_terms(feature_pad, grad_masked.reshape(-1, width), depth, width)
    weight_grad = lax.psum(local_grad, ("gx", "gy"))
    feature_grad = (backward_taps(grad_pad, weight, depth, width) * mask_flat).astype(jnp.bfloat16)
    out_rows = (output[flat_index].astype(jnp.float32) * got_valid).astype(jnp.bfloat16)
    grad_rows = feature_grad[flat_index]
    point_rows = jnp.dot(grad_rows, w_in.T, preferred_element_type=jnp.float32) * got_valid
    sent_point = point_rows.astype(jnp.bfloat16).reshape(shape_slots + (feat_width,))
    point_feat, point_grad = (
        lax.all_to_all(
            out_rows.reshape(shape_slots + (width,)), "gx", split_axis=2, concat_axis=2, tiled=True
        ),
        lax.all_to_all(sent_point, "gx", split_axis=2, concat_axis=2, tiled=True),
    )
    return (point_feat, point_grad, weight_grad)


def solution(mesh):
    placed = (
        P("gy", "gx", None, None, None),
        P("gy", "gx", None),
        P("gy", "gx", None, None),
        P("gx", "gy", None),
        P(),
        P(),
        P("gx", "gy", None, None),
    )
    return jax.shard_map(
        on_device,
        mesh=mesh,
        in_specs=placed,
        out_specs=(P("gy", "gx", None, None, None), P("gy", "gx", None, None, None), P()),
        check_vma=False,
    )
```

profile of v0, /device:TPU:1, one launch (start us, length us, event | category | flops | bytes accessed | tf_op | source)
XLA Modules:
  0.0 468.1 jit_solution(846735209724311216)
XLA Ops:
  7.2 1.4 copy.31
  8.5 15.1 %all-to-all-start.2 = ((s32[1,1,64]{1,0,2:T(1,128)}), s32[1,1,64]{1,0,2:T(1,128)S(1)}, u32[]{:S(2)}, u32[]{:S(2)}) async-start(s32[1,1,64]{1,0,2:T(1,128)} %copy.31), calls=%async_computation.2 | async-start | bytes 65536 | tf_op jit(solution)/shard_map/all_to_all | solution.py:64
  23.7 1.4 copy.29
  25.1 9.3 %all-to-all-done.2 = s32[1,1,64]{1,0,2:T(1,128)S(1)} async-done(((s32[1,1,64]{1,0,2:T(1,128)}), s32[1,1,64]{1,0,2:T(1,128)S(1)}, u32[]{:S(2)}, u32[]{:S(2)}) %all-to-all-start.2) | async-done | bytes 288 | tf_op jit(solution)/shard_map/all_to_all | solution.py:64
  34.4 4.6 all-to-all-start
  40.0 1.2 reduce.1
  41.4 8.4 %all-to-all-done = s32[1,1,64,32]{3,1,0,2:T(1,128)S(1)} async-done(((s32[1,1,64,32]{3,1,0,2:T(1,128)}), s32[1,1,64,32]{3,1,0,2:T(1,128)S(1)}, u32[]{:S(2)}, u32[]{:S(2)}) %all-to-all-start) | async-done | bytes 8224 | tf_op jit(solution)/shard_map/all_to_all | solution.py:63
  49.8 4.6 all-to-all-start.1
  55.9 13.2 %all-to-all-done.1 = bf16[1,1,64,32,128]{4,3,1,0,2:T(8,128)(2,1)S(1)} async-done(((bf16[1,1,64,32,128]{4,3,1,0,2:T(8,128)(2,1)}), bf16[1,1,64,32,128]{4,3,1,0,2:T(8,128)(2,1)S(1)}, u32[]{:S(2)}, u32[]{:S(2)}) %all-to-all-start.1) | async-done | bytes 524320 | tf_op jit(solution)/shard_map/all_to_all | solution.py:62
  69.8 11.6 %scatter_custom_fusion = f32[1024,96]{1,0:T(8,128)S(1)} fusion(s32[2048]{0:T(1024)S(1)} %bitcast.568, f32[2048,96]{1,0:T(8,128)S(1)} %copy.32, f32[]{:T(128)} %constant.1.clone.1), kind=kCustom, calls=%fused_computation.151 | custom fusion | flops 196608 | bytes 393220 | tf_op jit(solution)/shard_map/scatter-add | solution.py:75
  81.6 1.3 collective-permute-start.1
  82.9 5.5 %collective-permute-start = (bf16[1,8,16,96]{3,2,1,0:T(8,128)(2,1)S(1)}, bf16[1,8,16,96]{3,2,1,0:T(8,128)(2,1)S(1)}, u32[]{:S(2)}, u32[]{:S(2)}) collective-permute-start(bf16[1,8,16,96]{3,2,1,0:T(8,128)(2,1)S(1)} %get-tuple-element.71), channel_id=1, source_target_pairs={{0,4},{4,8},{8,12},{12,16},{16,20},{20,24},{24,28},{28,32},{32,36}... | collective-permute-start | bytes 73736 | tf_op jit(solution)/shard_map/ppermute | solution.py:12
  88.6 1.3 collective-permute-start.5
  89.9 5.5 %collective-permute-start.4 = (bf16[1,8,16,96]{3,2,1,0:T(8,128)(2,1)S(1)}, bf16[1,8,16,96]{3,2,1,0:T(8,128)(2,1)S(1)}, u32[]{:S(2)}, u32[]{:S(2)}) collective-permute-start(bf16[1,8,16,96]{3,2,1,0:T(8,128)(2,1)S(1)} %get-tuple-element.67), channel_id=1, source_target_pairs={{0,4},{4,8},{8,12},{12,16},{16,20},{20,24},{24,28},{28,32},{32,36}... | collective-permute-start | bytes 73736 | tf_op jit(solution)/shard_map/ppermute | solution.py:12
  95.4 8.8 %collective-permute-start.3 = (bf16[10,1,16,96]{3,2,1,0:T(8,128)(2,1)S(1)}, bf16[10,1,16,96]{3,2,1,0:T(8,128)(2,1)S(1)}, u32[]{:S(2)}, u32[]{:S(2)}) collective-permute-start(bf16[10,1,16,96]{3,2,1,0:T(8,128)(2,1)S(1)} %get-tuple-element.64), channel_id=1, source_target_pairs={{1,0},{2,1},{3,2},{5,4},{6,5},{7,6},{9,8},{10,9},{11,10},{13,12},{... | collective-permute-start | bytes 92168 | tf_op jit(solution)/shard_map/ppermute | solution.py:15
  104.2 2.1 collective-permute-start.2
  107.0 2.2 collective-permute-start.7
  109.2 3.5 collective-permute-start.6
  113.3 1.1 fusion.190
  122.1 6.2 %gather_fusion = bf16[2048,96]{1,0:T(8,128)(2,1)S(1)} fusion(bf16[1024,96]{1,0:T(8,128)(2,1)S(1)} %copy.34, s32[2048]{0:T(1024)S(1)} %broadcast_clamp_fusion), kind=kCustom, calls=%fused_computation | custom fusion | bytes 794624 | tf_op jit(solution)/shard_map/gather | solution.py:86
  128.3 1.1 fusion.39
  130.3 14.4 %all-to-all-start.3 = ((bf16[1,1,64,32,96]{4,3,1,0,2:T(8,128)(2,1)}), bf16[1,1,64,32,96]{4,3,1,0,2:T(8,128)(2,1)S(1)}, u32[]{:S(2)}, u32[]{:S(2)}) async-start(bf16[1,1,64,32,96]{4,3,1,0,2:T(8,128)(2,1)} %fusion.39), calls=%async_computation.3 | async-start | bytes 1048576 | tf_op jit(solution)/shard_map/all_to_all | solution.py:91
  145.0 1.1 fusion.189
  146.8 0.9 fusion.19
  147.7 0.9 fusion.37
  149.4 0.9 fusion.18
  150.3 0.9 fusion.35
  152.1 0.9 fusion.17
  152.9 0.9 fusion.33
  154.7 0.9 fusion.16
  155.6 0.9 fusion.31
  158.2 0.9 fusion.28
  159.9 0.9 fusion.15
  160.8 0.9 fusion.26
  162.6 0.9 fusion.14
  163.4 0.9 fusion.24
  170.3 0.9 fusion.23
  171.3 6.2 %gather_fusion.1 = bf16[2048,96]{1,0:T(8,128)(2,1)S(1)} fusion(bf16[1024,96]{1,0:T(8,128)(2,1)S(1)} %copy.36, s32[2048]{0:T(1024)S(1)} %broadcast_clamp_fusion), kind=kCustom, calls=%fused_computation.1 | custom fusion | bytes 794624 | tf_op jit(solution)/shard_map/gather | solution.py:87
  177.5 0.9 fusion.13
  178.4 0.9 fusion.22
  179.3 1.2 fusion
  180.4 11.9 %all-to-all-start.4 = ((bf16[1,1,64,32,128]{4,3,1,0,2:T(8,128)(2,1)}), bf16[1,1,64,32,128]{4,3,1,0,2:T(8,128)(2,1)S(1)}, u32[]{:S(2)}, u32[]{:S(2)}) async-start(bf16[1,1,64,32,128]{4,3,1,0,2:T(8,128)(2,1)} %bitcast.89), calls=%async_computation.4 | async-start | bytes 1048576 | tf_op jit(solution)/shard_map/all_to_all | solution.py:94
  192.4 0.9 fusion.21
  193.3 0.9 fusion.12
  194.2 0.9 fusion.20
  195.1 16.9 %all-to-all-done.4 = bf16[1,1,64,32,128]{4,3,1,0,2:T(8,128)(2,1)S(1)} async-done(((bf16[1,1,64,32,128]{4,3,1,0,2:T(8,128)(2,1)}), bf16[1,1,64,32,128]{4,3,1,0,2:T(8,128)(2,1)S(1)}, u32[]{:S(2)}, u32[]{:S(2)}) %all-to-all-start.4) | async-done | bytes 524320 | tf_op jit(solution)/shard_map/all_to_all | solution.py:94
  211.9 246.7 %all-reduce.4.cloned.1.call-done = f32[27,96,96]{2,1,0:T(8,128)} async-done(((f32[27,96,96]{2,1,0:T(8,128)}), f32[27,96,96]{2,1,0:T(8,128)}) %all-reduce.4.cloned.1.call-update) | async-done | bytes 995344 | tf_op jit(solution)/shard_map/psum | solution.py:84
  460.2 1.1 copy.98
  (117 shorter events, 28.0 us)
Async XLA Ops:
  7.2 61.9 %copy-start = (bf16[128,96]{0,1:T(8,128)(2,1)S(1)}, bf16[128,96]{0,1:T(8,128)(2,1)}, u32[]{:S(2)}) copy-start(bf16[128,96]{0,1:T(8,128)(2,1)} %param.12) | copy-start | bytes 73732
  8.5 25.9 %all-to-all-start.2 = ((s32[1,1,64]{1,0,2:T(1,128)}), s32[1,1,64]{1,0,2:T(1,128)S(1)}, u32[]{:S(2)}, u32[]{:S(2)}) async-start(s32[1,1,64]{1,0,2:T(1,128)} %copy.31), calls=%async_computation.2 | async-start | bytes 65536 | tf_op jit(solution)/shard_map/all_to_all | solution.py:64
  34.4 15.4 %all-to-all-start = ((s32[1,1,64,32]{3,1,0,2:T(1,128)}), s32[1,1,64,32]{3,1,0,2:T(1,128)S(1)}, u32[]{:S(2)}, u32[]{:S(2)}) async-start(s32[1,1,64,32]{3,1,0,2:T(1,128)} %copy.29), calls=%async_computation | async-start | bytes 65536 | tf_op jit(solution)/shard_map/all_to_all | solution.py:63
  49.8 19.3 %all-to-all-start.1 = ((bf16[1,1,64,32,128]{4,3,1,0,2:T(8,128)(2,1)}), bf16[1,1,64,32,128]{4,3,1,0,2:T(8,128)(2,1)S(1)}, u32[]{:S(2)}, u32[]{:S(2)}) async-start(bf16[1,1,64,32,128]{4,3,1,0,2:T(8,128)(2,1)} %bitcast.566), calls=%async_computation.1 | async-start | bytes 1048576 | tf_op jit(solution)/shard_map/all_to_all | solution.py:62
  69.4 12.0 %copy-start.3 = (bf16[8,8,16,96]{3,2,1,0:T(8,128)(2,1)S(1)}, bf16[8,8,16,96]{3,2,1,0:T(8,128)(2,1)}, u32[]{:S(2)}) copy-start(bf16[8,8,16,96]{3,2,1,0:T(8,128)(2,1)} %param.13) | copy-start | bytes 589828
  81.6 13.8 %collective-permute-start.1 = (bf16[1,8,16,96]{3,2,1,0:T(8,128)(2,1)S(1)}, bf16[1,8,16,96]{3,2,1,0:T(8,128)(2,1)S(1)}, u32[]{:S(2)}, u32[]{:S(2)}) collective-permute-start(bf16[1,8,16,96]{3,2,1,0:T(8,128)(2,1)S(1)} %get-tuple-element.72), channel_id=1, source_target_pairs={{4,0},{8,4},{12,8},{16,12},{20,16},{24,20},{28,24},{32,28},{36,32}... | collective-permute-start | bytes 73736 | tf_op jit(solution)/shard_map/ppermute | solution.py:15
  82.9 12.5 %collective-permute-start = (bf16[1,8,16,96]{3,2,1,0:T(8,128)(2,1)S(1)}, bf16[1,8,16,96]{3,2,1,0:T(8,128)(2,1)S(1)}, u32[]{:S(2)}, u32[]{:S(2)}) collective-permute-start(bf16[1,8,16,96]{3,2,1,0:T(8,128)(2,1)S(1)} %get-tuple-element.71), channel_id=1, source_target_pairs={{0,4},{4,8},{8,12},{12,16},{16,20},{20,24},{24,28},{28,32},{32,36}... | collective-permute-start | bytes 73736 | tf_op jit(solution)/shard_map/ppermute | solution.py:12
  88.6 17.8 %collective-permute-start.5 = (bf16[1,8,16,96]{3,2,1,0:T(8,128)(2,1)S(1)}, bf16[1,8,16,96]{3,2,1,0:T(8,128)(2,1)S(1)}, u32[]{:S(2)}, u32[]{:S(2)}) collective-permute-start(bf16[1,8,16,96]{3,2,1,0:T(8,128)(2,1)S(1)} %get-tuple-element.68), channel_id=1, source_target_pairs={{4,0},{8,4},{12,8},{16,12},{20,16},{24,20},{28,24},{32,28},{36,32}... | collective-permute-start | bytes 73736 | tf_op jit(solution)/shard_map/ppermute | solution.py:15
  89.9 16.5 %collective-permute-start.4 = (bf16[1,8,16,96]{3,2,1,0:T(8,128)(2,1)S(1)}, bf16[1,8,16,96]{3,2,1,0:T(8,128)(2,1)S(1)}, u32[]{:S(2)}, u32[]{:S(2)}) collective-permute-start(bf16[1,8,16,96]{3,2,1,0:T(8,128)(2,1)S(1)} %get-tuple-element.67), channel_id=1, source_target_pairs={{0,4},{4,8},{8,12},{12,16},{16,20},{20,24},{24,28},{28,32},{32,36}... | collective-permute-start | bytes 73736 | tf_op jit(solution)/shard_map/ppermute | solution.py:12
  95.4 17.5 %collective-permute-start.3 = (bf16[10,1,16,96]{3,2,1,0:T(8,128)(2,1)S(1)}, bf16[10,1,16,96]{3,2,1,0:T(8,128)(2,1)S(1)}, u32[]{:S(2)}, u32[]{:S(2)}) collective-permute-start(bf16[10,1,16,96]{3,2,1,0:T(8,128)(2,1)S(1)} %get-tuple-element.64), channel_id=1, source_target_pairs={{1,0},{2,1},{3,2},{5,4},{6,5},{7,6},{9,8},{10,9},{11,10},{13,12},{... | collective-permute-start | bytes 92168 | tf_op jit(solution)/shard_map/ppermute | solution.py:15
  104.2 8.7 %collective-permute-start.2 = (bf16[10,1,16,96]{3,2,1,0:T(8,128)(2,1)S(1)}, bf16[10,1,16,96]{3,2,1,0:T(8,128)(2,1)S(1)}, u32[]{:S(2)}, u32[]{:S(2)}) collective-permute-start(bf16[10,1,16,96]{3,2,1,0:T(8,128)(2,1)S(1)} %get-tuple-element.63), channel_id=1, source_target_pairs={{0,1},{1,2},{2,3},{4,5},{5,6},{6,7},{8,9},{9,10},{10,11},{12,13},{... | collective-permute-start | bytes 92168 | tf_op jit(solution)/shard_map/ppermute | solution.py:12
  107.0 37.7 %collective-permute-start.7 = (bf16[10,1,16,96]{3,2,1,0:T(8,128)(2,1)}, bf16[10,1,16,96]{3,2,1,0:T(8,128)(2,1)S(1)}, u32[]{:S(2)}, u32[]{:S(2)}) collective-permute-start(bf16[10,1,16,96]{3,2,1,0:T(8,128)(2,1)} %get-tuple-element.60), channel_id=1, source_target_pairs={{1,0},{2,1},{3,2},{5,4},{6,5},{7,6},{9,8},{10,9},{11,10},{13,12},{... | collective-permute-start | bytes 92168 | tf_op jit(solution)/shard_map/ppermute | solution.py:15
  109.2 35.5 %collective-permute-start.6 = (bf16[10,1,16,96]{3,2,1,0:T(8,128)(2,1)S(1)}, bf16[10,1,16,96]{3,2,1,0:T(8,128)(2,1)S(1)}, u32[]{:S(2)}, u32[]{:S(2)}) collective-permute-start(bf16[10,1,16,96]{3,2,1,0:T(8,128)(2,1)S(1)} %get-tuple-element.59), channel_id=1, source_target_pairs={{0,1},{1,2},{2,3},{4,5},{5,6},{6,7},{8,9},{9,10},{10,11},{12,13},{... | collective-permute-start | bytes 92168 | tf_op jit(solution)/shard_map/ppermute | solution.py:12
  113.3 1.1 copy-start.1
  130.3 50.1 %all-to-all-start.3 = ((bf16[1,1,64,32,96]{4,3,1,0,2:T(8,128)(2,1)}), bf16[1,1,64,32,96]{4,3,1,0,2:T(8,128)(2,1)S(1)}, u32[]{:S(2)}, u32[]{:S(2)}) async-start(bf16[1,1,64,32,96]{4,3,1,0,2:T(8,128)(2,1)} %fusion.39), calls=%async_computation.3 | async-start | bytes 1048576 | tf_op jit(solution)/shard_map/all_to_all | solution.py:91
  180.4 31.5 %all-to-all-start.4 = ((bf16[1,1,64,32,128]{4,3,1,0,2:T(8,128)(2,1)}), bf16[1,1,64,32,128]{4,3,1,0,2:T(8,128)(2,1)S(1)}, u32[]{:S(2)}, u32[]{:S(2)}) async-start(bf16[1,1,64,32,128]{4,3,1,0,2:T(8,128)(2,1)} %bitcast.89), calls=%async_computation.4 | async-start | bytes 1048576 | tf_op jit(solution)/shard_map/all_to_all | solution.py:94
  192.4 266.3 %all-reduce.4.cloned.1.call-start = ((), (), s32[]{:S(2)}) async-start(), calls=%async_computation.5 | async-start | bytes 2654208 | tf_op jit(solution)/shard_map/psum | solution.py:84
  458.6 1.6 copy-start.2
Sparse Core Ops, SparseCore 0:
  199.2 259.4 all-reduce.3
where the time goes:
time: 469 us; the launch traced here: 468 us
  waiting for transfers between devices  295 us (63%)
  starting transfers between devices  80.9 us (17%)
  matrix products  38.1 us (8%)
  local copies, waits for them, and re-layouts  22.7 us (5%)
  other arithmetic  17.2 us (4%)
  between operations  14.6 us (3%)
    psum x1, waiting for transfers between devices, on_device(): weight_grad = lax.psum(local_grad, ('gx', 'gy'))  247 us
    dot_general x27, matrix products, weight_terms(): lax.dot_general(window, grad_flat, (((0,), (0,)), ((), ())), preferred_el...  23.6 us
    all_to_all x1, waiting for transfers between devices, on_device(): lax.all_to_all(sent_point, 'gx', split_axis=2, concat_axis=2, tiled=True)  16.9 us
    ppermute x4, starting transfers between devices, padded_2(): lax.ppermute(lax.slice_in_dim(block, block.shape[dim] - width, None, axis...  16.6 us
    all_to_all x1, starting transfers between devices, on_device(): lax.all_to_all(counts, 'gx', split_axis=2, concat_axis=2, tiled=True)  15.1 us
    all_to_all x1, starting transfers between devices, on_device(): lax.all_to_all(out_rows.reshape(shape_slots + (width,)), 'gx', split_axis...  14.4 us
    ppermute x4, starting transfers between devices, padded_2(): lax.ppermute(lax.slice_in_dim(block, 0, width, axis=dim), axis, backward)  13.6 us
    all_to_all x1, waiting for transfers between devices, on_device(): lax.all_to_all(points, 'gx', split_axis=2, concat_axis=2, tiled=True)  13.2 us
  transfers between devices with their start and end apart: 14, of which 5 were waited for; matrix products, arithmetic and copies ran while one was open for 13% of the time, Pallas kernels for 0%

commit v1 on v0

--- a/solution.py
+++ b/solution.py
@@ -81,7 +81,7 @@
     mask_flat = mask.reshape(-1, 1)
     output = (forward_taps(feature_pad, weight, depth, width) * mask_flat).astype(jnp.bfloat16)
     local_grad = weight_terms(feature_pad, grad_masked.reshape(-1, width), depth, width)
-    weight_grad = lax.psum(local_grad, ("gx", "gy"))
+    weight_grad = lax.psum(lax.psum(local_grad, "gy"), "gx")
     feature_grad = (backward_taps(grad_pad, weight, depth, width) * mask_flat).astype(jnp.bfloat16)
     out_rows = (output[flat_index].astype(jnp.float32) * got_valid).astype(jnp.bfloat16)
     grad_rows = feature_grad[flat_index]

time: 469 us -> 923 us (1.97)
  the two profiles are of different devices: /device:TPU:1 before, /device:TPU:8 now
where the time goes in v1:
time: 923 us; the launch traced here: 922 us
  waiting for transfers between devices  747 us (81%)
  starting transfers between devices  76.2 us (8%)
  matrix products  38.8 us (4%)
  local copies, waits for them, and re-layouts  27.5 us (3%)
  other arithmetic  17.4 us (2%)
  between operations  14.7 us (2%)
    psum x2, waiting for transfers between devices, on_device(): weight_grad = lax.psum(lax.psum(local_grad, 'gy'), 'gx')  713 us
    dot_general x27, matrix products, weight_terms(): lax.dot_general(window, grad_flat, (((0,), (0,)), ((), ())), preferred_el...  23.6 us
  transfers between devices with their start and end apart: 15, of which 6 were waited for; matrix products, arithmetic and copies ran while one was open for 7% of the time, Pallas kernels for 0%

profile of v1, /device:TPU:8, one launch (start us, length us, event | category | flops | bytes accessed | tf_op | source)
XLA Modules:
  0.0 921.9 jit_solution(3263087479019215200)
XLA Ops:
  7.2 1.4 copy.31
  8.5 14.6 %all-to-all-start.2 = ((s32[1,1,64]{1,0,2:T(1,128)}), s32[1,1,64]{1,0,2:T(1,128)S(1)}, u32[]{:S(2)}, u32[]{:S(2)}) async-start(s32[1,1,64]{1,0,2:T(1,128)} %copy.31), calls=%async_computation.2 | async-start | bytes 65536 | tf_op jit(solution)/shard_map/all_to_all | solution.py:64
  23.1 1.4 copy.29
  24.5 9.5 %all-to-all-done.2 = s32[1,1,64]{1,0,2:T(1,128)S(1)} async-done(((s32[1,1,64]{1,0,2:T(1,128)}), s32[1,1,64]{1,0,2:T(1,128)S(1)}, u32[]{:S(2)}, u32[]{:S(2)}) %all-to-all-start.2) | async-done | bytes 288 | tf_op jit(solution)/shard_map/all_to_all | solution.py:64
  34.0 5.5 all-to-all-start
  40.5 1.2 reduce.1
  41.9 8.7 all-to-all-done
  50.6 5.5 all-to-all-start.1
  57.5 14.9 %all-to-all-done.1 = bf16[1,1,64,32,128]{4,3,1,0,2:T(8,128)(2,1)S(1)} async-done(((bf16[1,1,64,32,128]{4,3,1,0,2:T(8,128)(2,1)}), bf16[1,1,64,32,128]{4,3,1,0,2:T(8,128)(2,1)S(1)}, u32[]{:S(2)}, u32[]{:S(2)}) %all-to-all-start.1) | async-done | bytes 524320 | tf_op jit(solution)/shard_map/all_to_all | solution.py:62
  73.1 11.6 %scatter_custom_fusion = f32[1024,96]{1,0:T(8,128)S(1)} fusion(s32[2048]{0:T(1024)S(1)} %bitcast.568, f32[2048,96]{1,0:T(8,128)S(1)} %copy.32, f32[]{:T(128)} %constant.1.clone.1), kind=kCustom, calls=%fused_computation.151 | custom fusion | flops 196608 | bytes 393220 | tf_op jit(solution)/shard_map/scatter-add | solution.py:75
  84.9 3.6 collective-permute-start.1
  88.6 3.7 collective-permute-start
  92.5 4.5 collective-permute-start.5
  97.1 2.8 collective-permute-start.4
  99.9 1.3 collective-permute-start.3
  101.2 3.0 collective-permute-start.2
  104.3 1.0 collective-permute-done.4
  105.3 1.3 collective-permute-start.7
  106.6 3.2 collective-permute-start.6
  111.1 1.1 fusion.190
  119.9 6.2 gather_fusion
  126.1 1.1 fusion.39
  128.1 14.1 %all-to-all-start.3 = ((bf16[1,1,64,32,96]{4,3,1,0,2:T(8,128)(2,1)}), bf16[1,1,64,32,96]{4,3,1,0,2:T(8,128)(2,1)S(1)}, u32[]{:S(2)}, u32[]{:S(2)}) async-start(bf16[1,1,64,32,96]{4,3,1,0,2:T(8,128)(2,1)} %fusion.39), calls=%async_computation.3 | async-start | bytes 1048576 | tf_op jit(solution)/shard_map/all_to_all | solution.py:91
  142.8 2.0 fusion.189
  145.1 1.0 fusion.99
  146.2 0.9 fusion.19
  147.1 0.9 fusion.37
  148.9 0.9 fusion.18
  149.8 0.9 fusion.35
  151.5 0.9 fusion.17
  152.4 0.9 fusion.33
  154.1 0.9 fusion.16
  155.0 0.9 fusion.31
  157.6 0.9 fusion.28
  159.4 0.9 fusion.15
  160.2 0.9 fusion.26
  162.0 0.9 fusion.14
  162.9 0.9 fusion.24
  164.6 0.9 fusion.13
  165.5 0.9 fusion.22
  167.2 0.9 fusion.12
  168.1 0.9 fusion.20
  179.2 6.2 gather_fusion.1
  185.4 1.2 fusion
  186.5 12.7 %all-to-all-start.4 = ((bf16[1,1,64,32,128]{4,3,1,0,2:T(8,128)(2,1)}), bf16[1,1,64,32,128]{4,3,1,0,2:T(8,128)(2,1)S(1)}, u32[]{:S(2)}, u32[]{:S(2)}) async-start(bf16[1,1,64,32,128]{4,3,1,0,2:T(8,128)(2,1)} %bitcast.89), calls=%async_computation.4 | async-start | bytes 1048576 | tf_op jit(solution)/shard_map/all_to_all | solution.py:94
  199.3 22.4 %all-reduce.5.cloned.1.call-done = f32[27,96,96]{2,1,0:T(8,128)} async-done(((f32[27,96,96]{2,1,0:T(8,128)}), f32[27,96,96]{2,1,0:T(8,128)}) %all-reduce.5.cloned.1.call-update) | async-done | bytes 995344 | tf_op jit(solution)/shard_map/psum | solution.py:84
  221.7 690.7 %all-reduce.7.cloned.1.call-done = f32[27,96,96]{2,1,0:T(8,128)} async-done(((f32[27,96,96]{2,1,0:T(8,128)}), f32[27,96,96]{2,1,0:T(8,128)}) %all-reduce.7.cloned.1.call-update) | async-done | bytes 995344 | tf_op jit(solution)/shard_map/psum | solution.py:84
  914.0 1.1 copy.99
  (156 shorter events, 33.8 us)
Async XLA Ops:
  7.2 65.3 %copy-start = (bf16[128,96]{0,1:T(8,128)(2,1)S(1)}, bf16[128,96]{0,1:T(8,128)(2,1)}, u32[]{:S(2)}) copy-start(bf16[128,96]{0,1:T(8,128)(2,1)} %param.12) | copy-start | bytes 73732
  8.5 25.5 %all-to-all-start.2 = ((s32[1,1,64]{1,0,2:T(1,128)}), s32[1,1,64]{1,0,2:T(1,128)S(1)}, u32[]{:S(2)}, u32[]{:S(2)}) async-start(s32[1,1,64]{1,0,2:T(1,128)} %copy.31), calls=%async_computation.2 | async-start | bytes 65536 | tf_op jit(solution)/shard_map/all_to_all | solution.py:64
  34.0 16.5 %all-to-all-start = ((s32[1,1,64,32]{3,1,0,2:T(1,128)}), s32[1,1,64,32]{3,1,0,2:T(1,128)S(1)}, u32[]{:S(2)}, u32[]{:S(2)}) async-start(s32[1,1,64,32]{3,1,0,2:T(1,128)} %copy.29), calls=%async_computation | async-start | bytes 65536 | tf_op jit(solution)/shard_map/all_to_all | solution.py:63
  50.6 21.9 %all-to-all-start.1 = ((bf16[1,1,64,32,128]{4,3,1,0,2:T(8,128)(2,1)}), bf16[1,1,64,32,128]{4,3,1,0,2:T(8,128)(2,1)S(1)}, u32[]{:S(2)}, u32[]{:S(2)}) async-start(bf16[1,1,64,32,128]{4,3,1,0,2:T(8,128)(2,1)} %bitcast.566), calls=%async_computation.1 | async-start | bytes 1048576 | tf_op jit(solution)/shard_map/all_to_all | solution.py:62
  72.8 12.0 %copy-start.21 = (bf16[8,8,16,96]{3,2,1,0:T(8,128)(2,1)S(1)}, bf16[8,8,16,96]{3,2,1,0:T(8,128)(2,1)}, u32[]{:S(2)}) copy-start(bf16[8,8,16,96]{3,2,1,0:T(8,128)(2,1)} %param.13) | copy-start | bytes 589828
  84.9 14.9 %collective-permute-start.1 = (bf16[1,8,16,96]{3,2,1,0:T(8,128)(2,1)S(1)}, bf16[1,8,16,96]{3,2,1,0:T(8,128)(2,1)S(1)}, u32[]{:S(2)}, u32[]{:S(2)}) collective-permute-start(bf16[1,8,16,96]{3,2,1,0:T(8,128)(2,1)S(1)} %get-tuple-element.72), channel_id=1, source_target_pairs={{4,0},{8,4},{12,8},{16,12},{20,16},{24,20},{28,24},{32,28},{36,32}... | collective-permute-start | bytes 73736 | tf_op jit(solution)/shard_map/ppermute | solution.py:15
  88.6 11.3 %collective-permute-start = (bf16[1,8,16,96]{3,2,1,0:T(8,128)(2,1)S(1)}, bf16[1,8,16,96]{3,2,1,0:T(8,128)(2,1)S(1)}, u32[]{:S(2)}, u32[]{:S(2)}) collective-permute-start(bf16[1,8,16,96]{3,2,1,0:T(8,128)(2,1)S(1)} %get-tuple-element.71), channel_id=1, source_target_pairs={{0,4},{4,8},{8,12},{12,16},{16,20},{20,24},{24,28},{28,32},{32,36}... | collective-permute-start | bytes 73736 | tf_op jit(solution)/shard_map/ppermute | solution.py:12
  92.5 11.8 %collective-permute-start.5 = (bf16[1,8,16,96]{3,2,1,0:T(8,128)(2,1)S(1)}, bf16[1,8,16,96]{3,2,1,0:T(8,128)(2,1)S(1)}, u32[]{:S(2)}, u32[]{:S(2)}) collective-permute-start(bf16[1,8,16,96]{3,2,1,0:T(8,128)(2,1)S(1)} %get-tuple-element.68), channel_id=1, source_target_pairs={{4,0},{8,4},{12,8},{16,12},{20,16},{24,20},{28,24},{32,28},{36,32}... | collective-permute-start | bytes 73736 | tf_op jit(solution)/shard_map/ppermute | solution.py:15
  97.1 8.2 collective-permute-start.4
  99.9 10.8 %collective-permute-start.3 = (bf16[10,1,16,96]{3,2,1,0:T(8,128)(2,1)S(1)}, bf16[10,1,16,96]{3,2,1,0:T(8,128)(2,1)S(1)}, u32[]{:S(2)}, u32[]{:S(2)}) collective-permute-start(bf16[10,1,16,96]{3,2,1,0:T(8,128)(2,1)S(1)} %get-tuple-element.64), channel_id=1, source_target_pairs={{1,0},{2,1},{3,2},{5,4},{6,5},{7,6},{9,8},{10,9},{11,10},{13,12},{... | collective-permute-start | bytes 92168 | tf_op jit(solution)/shard_map/ppermute | solution.py:15
  101.2 9.5 %collective-permute-start.2 = (bf16[10,1,16,96]{3,2,1,0:T(8,128)(2,1)S(1)}, bf16[10,1,16,96]{3,2,1,0:T(8,128)(2,1)S(1)}, u32[]{:S(2)}, u32[]{:S(2)}) collective-permute-start(bf16[10,1,16,96]{3,2,1,0:T(8,128)(2,1)S(1)} %get-tuple-element.63), channel_id=1, source_target_pairs={{0,1},{1,2},{2,3},{4,5},{5,6},{6,7},{8,9},{9,10},{10,11},{12,13},{... | collective-permute-start | bytes 92168 | tf_op jit(solution)/shard_map/ppermute | solution.py:12
  105.3 37.2 %collective-permute-start.7 = (bf16[10,1,16,96]{3,2,1,0:T(8,128)(2,1)S(1)}, bf16[10,1,16,96]{3,2,1,0:T(8,128)(2,1)S(1)}, u32[]{:S(2)}, u32[]{:S(2)}) collective-permute-start(bf16[10,1,16,96]{3,2,1,0:T(8,128)(2,1)S(1)} %get-tuple-element.60), channel_id=1, source_target_pairs={{1,0},{2,1},{3,2},{5,4},{6,5},{7,6},{9,8},{10,9},{11,10},{13,12},{... | collective-permute-start | bytes 92168 | tf_op jit(solution)/shard_map/ppermute | solution.py:15
  106.6 35.9 %collective-permute-start.6 = (bf16[10,1,16,96]{3,2,1,0:T(8,128)(2,1)S(1)}, bf16[10,1,16,96]{3,2,1,0:T(8,128)(2,1)S(1)}, u32[]{:S(2)}, u32[]{:S(2)}) collective-permute-start(bf16[10,1,16,96]{3,2,1,0:T(8,128)(2,1)S(1)} %get-tuple-element.59), channel_id=1, source_target_pairs={{0,1},{1,2},{2,3},{4,5},{5,6},{6,7},{8,9},{9,10},{10,11},{12,13},{... | collective-permute-start | bytes 92168 | tf_op jit(solution)/shard_map/ppermute | solution.py:12
  111.1 1.1 copy-start.1
  128.1 58.4 %all-to-all-start.3 = ((bf16[1,1,64,32,96]{4,3,1,0,2:T(8,128)(2,1)}), bf16[1,1,64,32,96]{4,3,1,0,2:T(8,128)(2,1)S(1)}, u32[]{:S(2)}, u32[]{:S(2)}) async-start(bf16[1,1,64,32,96]{4,3,1,0,2:T(8,128)(2,1)} %fusion.39), calls=%async_computation.3 | async-start | bytes 1048576 | tf_op jit(solution)/shard_map/all_to_all | solution.py:91
  142.2 79.5 %all-reduce.5.cloned.1.call-start = ((), (), s32[]{:S(2)}) async-start(), calls=%async_computation.5 | async-start | bytes 2654208 | tf_op jit(solution)/shard_map/psum | solution.py:84
  169.1 1.0 copy-start.18
  169.4 1.0 copy-start.17
  169.7 1.0 copy-start.2
  169.7 1.1 copy-start.20
  170.3 1.0 copy-start.16
  171.0 1.0 copy-start.15
  171.6 1.0 copy-start.14
  172.2 1.0 copy-start.13
  172.7 1.0 copy-start.12
  173.4 1.0 copy-start.11
  173.9 1.0 copy-start.10
  174.6 1.0 copy-start.9
  175.1 1.0 copy-start.8
  175.8 1.0 copy-start.7
  176.3 1.0 copy-start.6
  176.6 1.0 copy-start.19
  177.0 1.0 copy-start.5
  177.8 1.0 copy-start.4
  186.5 35.2 %all-to-all-start.4 = ((bf16[1,1,64,32,128]{4,3,1,0,2:T(8,128)(2,1)}), bf16[1,1,64,32,128]{4,3,1,0,2:T(8,128)(2,1)S(1)}, u32[]{:S(2)}, u32[]{:S(2)}) async-start(bf16[1,1,64,32,128]{4,3,1,0,2:T(8,128)(2,1)} %bitcast.89), calls=%async_computation.4 | async-start | bytes 1048576 | tf_op jit(solution)/shard_map/all_to_all | solution.py:94
  199.2 713.2 %all-reduce.7.cloned.1.call-start = ((), (), s32[]{:S(2)}) async-start(), calls=%async_computation.6 | async-start | bytes 2654208 | tf_op jit(solution)/shard_map/psum | solution.py:84
  912.4 1.6 copy-start.3
Sparse Core Ops, SparseCore 0:
  169.1 52.5 all-reduce.4
  224.3 688.0 all-reduce.6
